TPU v7x, 512 devices: a whole 4x8x8 slice. The times are simulated.
512 devices in a mesh: slab: 128 (over y, z, core), case: 4 (over x).
Axes of the slice: x: 4, y: 8, z: 8, core: 2. Of those that a mesh axis runs over, the one named last changes fastest.
Arguments:
- pressure: float32 [64, 512], replicated, may hold values from -9 to 9
- panel: int32 [1536, 4, 128], P('slab'), may hold values from 0 to 511
- flags: int32 [1536, 4, 128], P('slab'), may hold values 0 or 1
- diagonal: float32 [1536, 4, 128], P('slab'), may hold values from 0.25 to 4
Outputs:
- fields: float32 [64, 1536, 4, 128], P('case', 'slab')
- gram: float32 [64, 64], P('case')
- cross: float32 [64, 64], P('case')
All inputs are finite; a program needn't handle non-finite values. No bound on the sum of `flags` on one device may be relied on, other than what follows from the above.
Results may differ from a plain program's by a relative error of at most 0.00005.
Values sent between devices are 32-bit elements; how exact they have to be, the bound alone decides.
A program may use at most 64 MiB of HBM per device.

v0:
```python
import jax
import jax.numpy as jnp
from jax import lax
from jax.sharding import PartitionSpec as P

damping = 0.7
penalty = 4.0
highest = lax.Precision.HIGHEST


def with_halo(cells, sides, width):
    for axis, dim in sides:
        count = lax.axis_size(axis)
        ends = count - 1
        head = lax.slice_in_dim(cells, 0, width, axis=dim)
        tail = lax.slice_in_dim(cells, cells.shape[dim] - width, cells.shape[dim], axis=dim)
        cells = jnp.concatenate(
            [
                lax.ppermute(tail, axis, [(i, (i + 1) % count) for i in range(ends)]),
                cells,
                lax.ppermute(head, axis, [((i + 1) % count, i) for i in range(ends)]),
            ],
            axis=dim,
        )
    return cells


def from_behind(x, axis, by):
    count = lax.axis_size(axis)
    pairs = [(i, i + by) for i in range(count) if 0 <= i + by < count]
    return lax.ppermute(x, axis, pairs)


def transverse(field):
    beside_all = jnp.roll(field, 1, axis=-1) + jnp.roll(field, -1, axis=-1)
    zero_row = jnp.zeros_like(field[..., :1, :])
    inward = jnp.concatenate([zero_row, field[..., :-1, :]], axis=-2)
    outward = jnp.concatenate([field[..., 1:, :], zero_row], axis=-2)
    return beside_all + inward + outward


def stencil(field, below, above, coeff, weight):
    return (coeff + 2.0 * weight + 4.0) * field - weight * (below + above) - transverse(field)


def apply_halo(field, coeff, weight):
    padded = with_halo(field, (("slab", 1),), 1)
    return stencil(field, padded[:, :-2], padded[:, 2:], coeff, weight)


def smooth_halo(field, rhs, coeff, weight):
    return field + damping * (rhs - apply_halo(field, coeff, weight)) / (coeff + 2.0 * weight + 4.0)


def restrict(fine):
    even = fine[:, 0::2]
    odd = fine[:, 1::2]
    lower = from_behind(fine[:, -1:], "slab", 1)
    odd_before = jnp.concatenate([lower, odd[:, :-1]], axis=1)
    return 0.5 * even + 0.25 * (odd + odd_before)


def prolong(coarse):
    upper = from_behind(coarse[:, :1], "slab", -1)
    following = jnp.concatenate([coarse[:, 1:], upper], axis=1)
    middle = 0.5 * (coarse + following)
    stacked = jnp.stack([coarse, middle], axis=2)
    shape = coarse.shape
    return stacked.reshape(shape[0], 2 * shape[1], shape[2], shape[3])


def coarsest(rhs, coeff, weight):
    field = damping * rhs / (coeff + 2.0 * weight + 4.0)
    for sweep in range(3):
        field = smooth_halo(field, rhs, coeff, weight)
    return field


def vcycle(rhs, coeff, level):
    weight = 0.25**level
    if level == 2:
        return coarsest(rhs, coeff, weight)
    field = damping * rhs / (coeff + 2.0 * weight + 4.0)
    field = smooth_halo(field, rhs, coeff, weight)
    leftover = rhs - apply_halo(field, coeff, weight)
    coarse_coeff = 0.5 * (coeff[0::2] + coeff[1::2])
    field = field + prolong(vcycle(restrict(leftover), coarse_coeff, level + 1))
    for sweep in range(2):
        field = smooth_halo(field, rhs, coeff, weight)
    return field


def local(pressure, panel, flags, diagonal):
    layers, radial, beside_all = panel.shape
    slabs = lax.axis_size("slab")
    groups = lax.axis_size("case")
    per_group = pressure.shape[0] // groups
    total_layers = layers * slabs
    own_group = lax.axis_index("case")
    case_rows = lax.dynamic_slice_in_dim(pressure, own_group * per_group, per_group, 0)
    coeff = diagonal + penalty * flags.astype(jnp.float32)
    keep = 1.0 - flags.astype(jnp.float32)
    positions = (lax.axis_index("slab") * layers + jnp.arange(layers)).astype(jnp.float32)
    span = (1.0 + 2.0 * positions / total_layers)[:, None, None]
    loads = jnp.take(case_rows, panel, axis=1) * span * keep
    fields = vcycle(loads, coeff, 0)
    images = apply_halo(fields, coeff, 1.0)
    scale = 1.0 / (total_layers * radial * beside_all)
    contract = (((1,), (1,)), ((), ()))
    images_flat = images.reshape(per_group, -1)
    loads_flat = loads.reshape(per_group, -1)
    piece = lax.all_gather(fields, "case", axis=0, tiled=True)
    piece_flat = piece.reshape(piece.shape[0], -1)
    gram_block = lax.dot_general(
        images_flat, piece_flat, contract, precision=highest, preferred_element_type=jnp.float32
    )
    cross_block = lax.dot_general(
        loads_flat, piece_flat, contract, precision=highest, preferred_element_type=jnp.float32
    )
    gram_rows, cross_rows = lax.psum((gram_block, cross_block), "slab")
    return (fields, gram_rows * scale, cross_rows * scale)


def solution(mesh):
    in_specs = (P(), P("slab", None, None), P("slab", None, None), P("slab", None, None))
    out_specs = (P("case", "slab", None, None), P("case", None), P("case", None))
    return jax.shard_map(local, mesh=mesh, in_specs=in_specs, out_specs=out_specs, check_vma=False)
```

profile of v0, /device:TPU:2, one launch (start us, length us, event | category | flops | bytes accessed | tf_op | source)
XLA Modules:
  0.0 730.1 jit_solution(7467663255318855311)
XLA Ops:
  8.9 20.9 %gather_fusion = f32[6144,16]{1,0:T(8,128)} fusion(f32[16,512]{0,1:T(8,128)S(1)} %copy.21, s32[6144]{0:T(1024)S(1)} %broadcast_clamp_fusion), kind=kCustom, calls=%fused_computation | custom fusion | bytes 811008 | tf_op jit(solution)/shard_map/jit(_take)/gather | solution.py:105
  29.9 2.3 copy.13
  32.4 1.7 collective-permute-start
  34.2 1.3 collective-permute-start.1
  35.9 3.5 collective-permute-done.1
  40.3 4.5 collective-permute-start.2
  44.8 1.3 collective-permute-start.3
  46.2 1.7 collective-permute-done.3
  48.4 4.8 collective-permute-start.4
  54.3 2.3 collective-permute-start.5
  56.6 1.3 collective-permute-start.6
  57.9 3.4 collective-permute-done.6
  61.8 4.5 collective-permute-start.7
  66.3 1.3 collective-permute-start.8
  67.6 3.5 collective-permute-done.8
  71.4 5.4 collective-permute-start.9
  77.9 2.3 collective-permute-start.10
  80.2 1.3 collective-permute-start.11
  81.5 3.9 collective-permute-done.11
  85.7 4.5 collective-permute-start.12
  90.3 1.3 collective-permute-start.13
  91.6 3.6 collective-permute-done.13
  95.5 5.4 collective-permute-start.14
  100.9 1.3 collective-permute-start.15
  102.3 1.8 collective-permute-done.15
  104.2 1.3 collective-permute-start.16
  105.5 4.6 collective-permute-done.16
  110.5 4.5 collective-permute-start.17
  115.0 1.3 collective-permute-start.18
  116.4 3.5 collective-permute-done.18
  120.4 5.4 collective-permute-start.19
  125.8 1.3 collective-permute-start.20
  127.1 1.8 collective-permute-done.20
  129.1 1.3 collective-permute-start.21
  130.4 4.6 collective-permute-done.21
  135.6 4.5 collective-permute-start.22
  140.2 1.3 collective-permute-start.23
  141.5 2.8 collective-permute-done.23
  145.2 5.4 collective-permute-start.24
  150.6 1.3 collective-permute-start.25
  152.0 1.7 collective-permute-done.25
  155.0 1.9 copy.16
  157.7 5.3 collective-permute-start.26
  162.9 1.3 collective-permute-start.27
  164.7 57.1 %all-gather.2.cloned.1.call-done = f32[64,12,4,128]{3,0,2,1:T(8,128)} async-done(((f32[16,12,4,128]{3,0,2,1:T(8,128)}), f32[64,12,4,128]{3,0,2,1:T(8,128)}) %all-gather.2.cloned.1.call-update) | async-done | bytes 1572880 | tf_op jit(solution)/shard_map/all_gather | solution.py:112
  221.8 2.9 convolution_bitcast_fusion
  224.7 1.4 convolution_bitcast_fusion.1
  226.2 496.5 %all-reduce.24 = (f32[16,64]{1,0:T(8,128)S(1)}, f32[16,64]{1,0:T(8,128)S(1)}) all-reduce(f32[16,64]{1,0:T(8,128)S(1)} %convolution_bitcast_fusion.1, f32[16,64]{1,0:T(8,128)S(1)} %convolution_bitcast_fusion), channel_id=1, replica_groups=mesh['slab'=128,'case'=4] {'slab'}, use_global_device_ids=true, to_apply=%region_0.1 | all-reduce | flops 2048 | bytes 16384 | tf_op jit(solution)/shard_map/psum | solution.py:120
  (117 shorter events, 12.7 us)
Async XLA Ops:
  7.2 1.6 copy-start
  7.2 214.6 %all-gather.2.cloned.1.call-start = ((), (), s32[]{:S(2)}) async-start(), calls=%async_computation | async-start | bytes 1966080 | tf_op jit(solution)/shard_map/all_gather | solution.py:112
  29.9 2.3 copy-start.3
  29.9 2.4 copy-start.4
  32.4 3.5 collective-permute-start
  34.2 5.3 collective-permute-start.1
  40.3 5.9 collective-permute-start.2
  44.8 3.1 collective-permute-start.3
  48.4 5.6 collective-permute-start.4
  54.3 3.6 collective-permute-start.5
  56.6 4.8 collective-permute-start.6
  61.8 5.9 collective-permute-start.7
  66.3 4.9 collective-permute-start.8
  71.4 6.3 collective-permute-start.9
  77.9 3.6 collective-permute-start.10
  80.2 5.2 collective-permute-start.11
  85.7 5.9 collective-permute-start.12
  90.3 4.9 collective-permute-start.13
  95.5 6.8 collective-permute-start.14
  100.9 3.1 collective-permute-start.15
  104.2 6.0 collective-permute-start.16
  110.5 5.9 collective-permute-start.17
  115.0 4.9 collective-permute-start.18
  120.4 6.8 collective-permute-start.19
  125.8 3.1 collective-permute-start.20
  129.1 6.0 collective-permute-start.21
  135.6 5.9 collective-permute-start.22
  140.2 4.1 collective-permute-start.23
  145.2 6.8 collective-permute-start.24
  150.6 3.1 collective-permute-start.25
  154.9 9.3 %copy-start.1 = (f32[16,12,4,128]{3,0,2,1:T(8,128)S(1)}, f32[16,12,4,128]{3,0,2,1:T(8,128)}, u32[]{:S(2)}) copy-start(f32[16,12,4,128]{3,0,2,1:T(8,128)} %fusion.12) | copy-start | bytes 1179652
  157.7 67.0 %collective-permute-start.26 = (f32[16,1,4,128]{3,0,2,1:T(8,128)S(1)}, f32[16,1,4,128]{3,0,2,1:T(8,128)S(1)}, u32[]{:S(2)}, u32[]{:S(2)}) collective-permute-start(f32[16,1,4,128]{3,0,2,1:T(8,128)S(1)} %get-tuple-element.25), channel_id=1, source_target_pairs={{0,4},{4,8},{8,12},{12,16},{16,20},{20,24},{24,28},{28,32},{32,36}... | collective-permute-start | bytes 98312 | tf_op jit(solution)/shard_map/ppermute | solution.py:19
  162.9 61.8 %collective-permute-start.27 = (f32[16,1,4,128]{3,0,2,1:T(8,128)S(1)}, f32[16,1,4,128]{3,0,2,1:T(8,128)S(1)}, u32[]{:S(2)}, u32[]{:S(2)}) collective-permute-start(f32[16,1,4,128]{3,0,2,1:T(8,128)S(1)} %get-tuple-element.26), channel_id=1, source_target_pairs={{4,0},{8,4},{12,8},{16,12},{20,16},{24,20},{28,24},{32,28},{36,32}... | collective-permute-start | bytes 98312 | tf_op jit(solution)/shard_map/ppermute | solution.py:21
  221.8 2.9 copy-start.2
Sparse Core Ops, SparseCore 0:
  155.1 66.6 all-gather.1
where the time goes:
time: 731 us; the launch traced here: 730 us
  blocking collectives  497 us (68%)
  waiting for transfers between devices  99.3 us (14%)
  starting transfers between devices  78.8 us (11%)
  local copies, waits for them, and re-layouts  29.9 us (4%)
  between operations  14.9 us (2%)
    psum x1, blocking collectives, local(): gram_rows, cross_rows = lax.psum((gram_block, cross_block), 'slab')  497 us
    all_gather x1, waiting for transfers between devices, local(): piece = lax.all_gather(fields, 'case', axis=0, tiled=True)  57.1 us
    ppermute x12, starting transfers between devices, with_halo(): lax.ppermute(tail, axis, [(i, (i + 1) % count) for i in range(ends)])  50.5 us
    ppermute x12, waiting for transfers between devices, with_halo(): lax.ppermute(head, axis, [((i + 1) % count, i) for i in range(ends)])  31.3 us
    gather x2, local copies, waits for them, and re-layouts, local(): loads = jnp.take(case_rows, panel, axis=1) * span * keep  23.3 us
    ppermute x12, starting transfers between devices, with_halo(): lax.ppermute(head, axis, [((i + 1) % count, i) for i in range(ends)])  15.5 us
  transfers between devices with their start and end apart: 29, of which 16 were waited for; matrix products, arithmetic and copies ran while one was open for 1% of the time, Pallas kernels for 0%

commit v1 on v0

--- a/solution.py
+++ b/solution.py
@@ -6,6 +6,12 @@
 damping = 0.7
 penalty = 4.0
 highest = lax.Precision.HIGHEST
+
+
+def joined_along(parts, dim):
+    parts = jnp.moveaxis(parts, 0, dim)
+    lengths = parts.shape
+    return parts.reshape(*lengths[:dim], lengths[dim] * lengths[dim + 1], *lengths[dim + 2 :])
 
 
 def with_halo(cells, sides, width):
@@ -109,7 +115,19 @@
     contract = (((1,), (1,)), ((), ()))
     images_flat = images.reshape(per_group, -1)
     loads_flat = loads.reshape(per_group, -1)
-    piece = lax.all_gather(fields, "case", axis=0, tiled=True)
+    length = lax.axis_size("case")
+    pairs_2 = [(i_2, (i_2 + 1) % length) for i_2 in range(length)]
+    back = [(b, a) for a, b in pairs_2]
+    lower_2, upper_2 = ([], [])
+    for lap in range(length - 1):
+        if lap % 2 == 0:
+            lower_2.append(lax.ppermute(lower_2[-1] if lower_2 else fields, "case", pairs_2))
+        else:
+            upper_2.append(lax.ppermute(upper_2[-1] if upper_2 else fields, "case", back))
+    tiles = jnp.stack([*lower_2[::-1], fields, *upper_2])
+    shift = lax.axis_index("case") - len(lower_2)
+    tiles = tiles[(jnp.arange(length) - shift) % length]
+    piece = joined_along(tiles, 0)
     piece_flat = piece.reshape(piece.shape[0], -1)
     gram_block = lax.dot_general(
         images_flat, piece_flat, contract, precision=highest, preferred_element_type=jnp.float32

time: 731 us -> 722 us (0.988)
  the two profiles are of different devices: /device:TPU:2 before, /device:TPU:32 now
where the time goes in v1:
time: 722 us; the launch traced here: 721 us
  blocking collectives  491 us (68%)
  waiting for transfers between devices  95.1 us (13%)
  starting transfers between devices  85.3 us (12%)
  local copies, waits for them, and re-layouts  34.8 us (5%)
  other arithmetic  10.6 us (1%)
    psum x1, blocking collectives, local(): gram_rows, cross_rows = lax.psum((gram_block, cross_block), 'slab')  491 us
    ppermute x12, waiting for transfers between devices, with_halo(): lax.ppermute(tail, axis, [(i, (i + 1) % count) for i in range(ends)])  67 us
    ppermute x12, starting transfers between devices, with_halo(): lax.ppermute(head, axis, [((i + 1) % count, i) for i in range(ends)])  41.5 us
    ppermute x12, starting transfers between devices, with_halo(): lax.ppermute(tail, axis, [(i, (i + 1) % count) for i in range(ends)])  27.6 us
    gather x2, local copies, waits for them, and re-layouts, local(): loads = jnp.take(case_rows, panel, axis=1) * span * keep  23.3 us
    ppermute x4, waiting for transfers between devices, from_behind(): return lax.ppermute(x, axis, pairs)  16 us
  transfers between devices with their start and end apart: 31, of which 17 were waited for; matrix products, arithmetic and copies ran while one was open for 0% of the time, Pallas kernels for 0%

profile of v1, /device:TPU:32, one launch (start us, length us, event | category | flops | bytes accessed | tf_op | source)
XLA Modules:
  0.0 720.9 jit_solution(17344483461186472931)
XLA Ops:
  2.4 21.0 %gather_fusion = f32[6144,16]{1,0:T(8,128)} fusion(f32[16,512]{0,1:T(8,128)S(1)} %copy.11, s32[6144]{0:T(1024)S(1)} %broadcast_clamp_fusion), kind=kCustom, calls=%fused_computation | custom fusion | bytes 811008 | tf_op jit(solution)/shard_map/jit(_take)/gather | solution.py:111
  23.4 2.3 copy.8
  26.0 10.3 %collective-permute-start.1 = (f32[16,1,4,128]{3,2,1,0:T(4,128)S(1)}, f32[16,1,4,128]{3,2,1,0:T(4,128)S(1)}, u32[]{:S(2)}, u32[]{:S(2)}) collective-permute-start(f32[16,1,4,128]{3,2,1,0:T(4,128)S(1)} %get-tuple-element.54), channel_id=1, source_target_pairs={{4,0},{8,4},{12,8},{16,12},{20,16},{24,20},{28,24},{32,28},{36,32}... | collective-permute-start | bytes 98312 | tf_op jit(solution)/shard_map/ppermute | solution.py:27
  36.3 1.9 collective-permute-start
  38.9 5.9 collective-permute-done
  48.1 2.4 collective-permute-start.2
  50.7 6.0 collective-permute-done.2
  57.4 1.9 collective-permute-start.4
  59.4 6.5 collective-permute-done.4
  66.5 1.9 collective-permute-start.6
  68.4 2.4 collective-permute-start.5
  70.9 6.0 collective-permute-done.5
  77.8 1.9 collective-permute-start.8
  79.7 2.4 collective-permute-start.7
  82.2 6.0 collective-permute-done.7
  88.7 1.9 collective-permute-start.9
  90.6 6.6 collective-permute-done.9
  97.5 1.9 collective-permute-start.11
  99.5 2.4 collective-permute-start.10
  101.9 6.1 collective-permute-done.10
  108.5 1.9 collective-permute-start.13
  110.4 2.4 collective-permute-start.12
  112.9 6.1 collective-permute-done.12
  119.5 1.9 collective-permute-start.15
  121.4 2.4 collective-permute-start.14
  123.9 6.1 collective-permute-done.14
  130.2 1.9 collective-permute-start.16
  134.3 7.0 collective-permute-start.18
  141.2 1.9 collective-permute-start.17
  143.3 6.5 collective-permute-done.17
  150.6 1.9 collective-permute-start.20
  152.5 2.4 collective-permute-start.19
  155.0 6.0 collective-permute-done.19
  161.5 1.9 collective-permute-start.21
  165.9 7.0 collective-permute-start.23
  172.9 2.1 collective-permute-start.22
  175.2 6.3 collective-permute-done.22
  184.7 2.4 collective-permute-start.24
  187.3 6.0 collective-permute-done.24
  194.1 4.7 collective-permute-start.30
  198.8 1.9 collective-permute-start.28
  200.7 1.9 collective-permute-start.27
  202.7 2.4 collective-permute-start.26
  205.6 4.1 collective-permute-done.28
  212.7 8.0 %collective-permute-done.29 = f32[16,12,4,128]{3,2,1,0:T(4,128)} collective-permute-done((f32[16,12,4,128]{3,2,1,0:T(4,128)S(1)}, f32[16,12,4,128]{3,2,1,0:T(4,128)}, u32[]{:S(2)}, u32[]{:S(2)}) %collective-permute-start.29) | collective-permute-done | bytes 393248 | tf_op jit(solution)/shard_map/ppermute | solution.py:124
  222.2 2.5 gather_fusion.1
  224.7 2.0 reshape_reshape.3
  229.4 491.0 %all-reduce.24 = (f32[16,64]{1,0:T(8,128)S(1)}, f32[16,64]{1,0:T(8,128)S(1)}) all-reduce(f32[16,64]{1,0:T(8,128)S(1)} %fusion.147, f32[16,64]{1,0:T(8,128)S(1)} %fusion.148), channel_id=1, replica_groups=mesh['slab'=128,'case'=4] {'slab'}, use_global_device_ids=true, to_apply=%region_0.1 | all-reduce | flops 2048 | bytes 16384 | tf_op jit(solution)/shard_map/psum | solution.py:138
  (127 shorter events, 28.8 us)
Async XLA Ops:
  0.6 1.6 copy-start
  23.4 2.4 copy-start.3
  23.4 2.4 copy-start.4
  26.0 12.9 %collective-permute-start.1 = (f32[16,1,4,128]{3,2,1,0:T(4,128)S(1)}, f32[16,1,4,128]{3,2,1,0:T(4,128)S(1)}, u32[]{:S(2)}, u32[]{:S(2)}) collective-permute-start(f32[16,1,4,128]{3,2,1,0:T(4,128)S(1)} %get-tuple-element.54), channel_id=1, source_target_pairs={{4,0},{8,4},{12,8},{16,12},{20,16},{24,20},{28,24},{32,28},{36,32}... | collective-permute-start | bytes 98312 | tf_op jit(solution)/shard_map/ppermute | solution.py:27
  36.3 8.6 %collective-permute-start = (f32[16,1,4,128]{3,2,1,0:T(4,128)S(1)}, f32[16,1,4,128]{3,2,1,0:T(4,128)S(1)}, u32[]{:S(2)}, u32[]{:S(2)}) collective-permute-start(f32[16,1,4,128]{3,2,1,0:T(4,128)S(1)} %get-tuple-element.53), channel_id=1, source_target_pairs={{0,4},{4,8},{8,12},{12,16},{16,20},{20,24},{24,28},{28,32},{32,36}... | collective-permute-start | bytes 98312 | tf_op jit(solution)/shard_map/ppermute | solution.py:25
  46.2 4.5 collective-permute-start.3
  48.1 8.6 %collective-permute-start.2 = (f32[16,1,4,128]{3,2,1,0:T(4,128)S(1)}, f32[16,1,4,128]{3,2,1,0:T(4,128)S(1)}, u32[]{:S(2)}, u32[]{:S(2)}) collective-permute-start(f32[16,1,4,128]{3,2,1,0:T(4,128)S(1)} %get-tuple-element.45), channel_id=1, source_target_pairs={{0,4},{4,8},{8,12},{12,16},{16,20},{20,24},{24,28},{28,32},{32,36}... | collective-permute-start | bytes 98312 | tf_op jit(solution)/shard_map/ppermute | solution.py:25
  57.4 8.6 %collective-permute-start.4 = (f32[16,1,4,128]{3,2,1,0:T(4,128)S(1)}, f32[16,1,4,128]{3,2,1,0:T(4,128)S(1)}, u32[]{:S(2)}, u32[]{:S(2)}) collective-permute-start(f32[16,1,4,128]{3,2,1,0:T(4,128)S(1)} %slice.600), channel_id=1, source_target_pairs={{0,4},{4,8},{8,12},{12,16},{16,20},{20,24},{24,28},{28,32},{32,36}... | collective-permute-start | bytes 98312 | tf_op jit(solution)/shard_map/ppermute | solution.py:37
  66.5 4.4 collective-permute-start.6
  68.4 8.6 %collective-permute-start.5 = (f32[16,1,4,128]{3,2,1,0:T(4,128)S(1)}, f32[16,1,4,128]{3,2,1,0:T(4,128)S(1)}, u32[]{:S(2)}, u32[]{:S(2)}) collective-permute-start(f32[16,1,4,128]{3,2,1,0:T(4,128)S(1)} %get-tuple-element.85), channel_id=1, source_target_pairs={{0,4},{4,8},{8,12},{12,16},{16,20},{20,24},{24,28},{28,32},{32,36}... | collective-permute-start | bytes 98312 | tf_op jit(solution)/shard_map/ppermute | solution.py:25
  77.8 4.4 collective-permute-start.8
  79.7 8.6 %collective-permute-start.7 = (f32[16,1,4,128]{3,2,1,0:T(4,128)S(1)}, f32[16,1,4,128]{3,2,1,0:T(4,128)S(1)}, u32[]{:S(2)}, u32[]{:S(2)}) collective-permute-start(f32[16,1,4,128]{3,2,1,0:T(4,128)S(1)} %get-tuple-element.77), channel_id=1, source_target_pairs={{0,4},{4,8},{8,12},{12,16},{16,20},{20,24},{24,28},{28,32},{32,36}... | collective-permute-start | bytes 98312 | tf_op jit(solution)/shard_map/ppermute | solution.py:25
  88.7 8.6 %collective-permute-start.9 = (f32[16,1,4,128]{3,2,1,0:T(4,128)S(1)}, f32[16,1,4,128]{3,2,1,0:T(4,128)S(1)}, u32[]{:S(2)}, u32[]{:S(2)}) collective-permute-start(f32[16,1,4,128]{3,2,1,0:T(4,128)S(1)} %slice.618), channel_id=1, source_target_pairs={{0,4},{4,8},{8,12},{12,16},{16,20},{20,24},{24,28},{28,32},{32,36}... | collective-permute-start | bytes 98312 | tf_op jit(solution)/shard_map/ppermute | solution.py:37
  97.5 4.4 collective-permute-start.11
  99.5 8.6 %collective-permute-start.10 = (f32[16,1,4,128]{3,2,1,0:T(4,128)S(1)}, f32[16,1,4,128]{3,2,1,0:T(4,128)S(1)}, u32[]{:S(2)}, u32[]{:S(2)}) collective-permute-start(f32[16,1,4,128]{3,2,1,0:T(4,128)S(1)} %get-tuple-element.109), channel_id=1, source_target_pairs={{0,4},{4,8},{8,12},{12,16},{16,20},{20,24},{24,28},{28,32},{32,36}... | collective-permute-start | bytes 98312 | tf_op jit(solution)/shard_map/ppermute | solution.py:25
  108.5 4.4 collective-permute-start.13
  110.4 8.6 %collective-permute-start.12 = (f32[16,1,4,128]{3,2,1,0:T(4,128)S(1)}, f32[16,1,4,128]{3,2,1,0:T(4,128)S(1)}, u32[]{:S(2)}, u32[]{:S(2)}) collective-permute-start(f32[16,1,4,128]{3,2,1,0:T(4,128)S(1)} %get-tuple-element.101), channel_id=1, source_target_pairs={{0,4},{4,8},{8,12},{12,16},{16,20},{20,24},{24,28},{28,32},{32,36}... | collective-permute-start | bytes 98312 | tf_op jit(solution)/shard_map/ppermute | solution.py:25
  119.5 4.4 collective-permute-start.15
  121.4 8.6 %collective-permute-start.14 = (f32[16,1,4,128]{3,2,1,0:T(4,128)S(1)}, f32[16,1,4,128]{3,2,1,0:T(4,128)S(1)}, u32[]{:S(2)}, u32[]{:S(2)}) collective-permute-start(f32[16,1,4,128]{3,2,1,0:T(4,128)S(1)} %get-tuple-element.93), channel_id=1, source_target_pairs={{0,4},{4,8},{8,12},{12,16},{16,20},{20,24},{24,28},{28,32},{32,36}... | collective-permute-start | bytes 98312 | tf_op jit(solution)/shard_map/ppermute | solution.py:25
  130.2 3.5 collective-permute-start.16
  134.3 9.0 %collective-permute-start.18 = (f32[16,1,4,128]{3,2,1,0:T(4,128)S(1)}, f32[16,1,4,128]{3,2,1,0:T(4,128)S(1)}, u32[]{:S(2)}, u32[]{:S(2)}) collective-permute-start(f32[16,1,4,128]{3,2,1,0:T(4,128)S(1)} %get-tuple-element.70), channel_id=1, source_target_pairs={{4,0},{8,4},{12,8},{16,12},{20,16},{24,20},{28,24},{32,28},{36,32}... | collective-permute-start | bytes 98312 | tf_op jit(solution)/shard_map/ppermute | solution.py:27
  141.2 8.6 %collective-permute-start.17 = (f32[16,1,4,128]{3,2,1,0:T(4,128)S(1)}, f32[16,1,4,128]{3,2,1,0:T(4,128)S(1)}, u32[]{:S(2)}, u32[]{:S(2)}) collective-permute-start(f32[16,1,4,128]{3,2,1,0:T(4,128)S(1)} %get-tuple-element.69), channel_id=1, source_target_pairs={{0,4},{4,8},{8,12},{12,16},{16,20},{20,24},{24,28},{28,32},{32,36}... | collective-permute-start | bytes 98312 | tf_op jit(solution)/shard_map/ppermute | solution.py:25
  150.6 4.4 collective-permute-start.20
  152.5 8.6 %collective-permute-start.19 = (f32[16,1,4,128]{3,2,1,0:T(4,128)S(1)}, f32[16,1,4,128]{3,2,1,0:T(4,128)S(1)}, u32[]{:S(2)}, u32[]{:S(2)}) collective-permute-start(f32[16,1,4,128]{3,2,1,0:T(4,128)S(1)} %get-tuple-element.61), channel_id=1, source_target_pairs={{0,4},{4,8},{8,12},{12,16},{16,20},{20,24},{24,28},{28,32},{32,36}... | collective-permute-start | bytes 98312 | tf_op jit(solution)/shard_map/ppermute | solution.py:25
  161.5 3.5 collective-permute-start.21
  165.9 9.2 %collective-permute-start.23 = (f32[16,1,4,128]{3,2,1,0:T(4,128)S(1)}, f32[16,1,4,128]{3,2,1,0:T(4,128)S(1)}, u32[]{:S(2)}, u32[]{:S(2)}) collective-permute-start(f32[16,1,4,128]{3,2,1,0:T(4,128)S(1)} %get-tuple-element.38), channel_id=1, source_target_pairs={{4,0},{8,4},{12,8},{16,12},{20,16},{24,20},{28,24},{32,28},{36,32}... | collective-permute-start | bytes 98312 | tf_op jit(solution)/shard_map/ppermute | solution.py:27
  172.9 8.6 %collective-permute-start.22 = (f32[16,1,4,128]{3,2,1,0:T(4,128)S(1)}, f32[16,1,4,128]{3,2,1,0:T(4,128)S(1)}, u32[]{:S(2)}, u32[]{:S(2)}) collective-permute-start(f32[16,1,4,128]{3,2,1,0:T(4,128)S(1)} %get-tuple-element.37), channel_id=1, source_target_pairs={{0,4},{4,8},{8,12},{12,16},{16,20},{20,24},{24,28},{28,32},{32,36}... | collective-permute-start | bytes 98312 | tf_op jit(solution)/shard_map/ppermute | solution.py:25
  182.8 4.5 collective-permute-start.25
  184.7 8.6 %collective-permute-start.24 = (f32[16,1,4,128]{3,2,1,0:T(4,128)S(1)}, f32[16,1,4,128]{3,2,1,0:T(4,128)S(1)}, u32[]{:S(2)}, u32[]{:S(2)}) collective-permute-start(f32[16,1,4,128]{3,2,1,0:T(4,128)S(1)} %get-tuple-element.29), channel_id=1, source_target_pairs={{0,4},{4,8},{8,12},{12,16},{16,20},{20,24},{24,28},{28,32},{32,36}... | collective-permute-start | bytes 98312 | tf_op jit(solution)/shard_map/ppermute | solution.py:25
  194.1 26.6 %copy-start.1 = (f32[16,12,4,128]{3,2,1,0:T(4,128)}, f32[16,12,4,128]{3,2,1,0:T(4,128)S(1)}, u32[]{:S(2)}) copy-start(f32[16,12,4,128]{3,2,1,0:T(4,128)S(1)} %divide_add_fusion) | copy-start | bytes 1179652
  194.1 18.5 %collective-permute-start.30 = (f32[16,12,4,128]{3,2,1,0:T(4,128)S(1)}, f32[16,12,4,128]{3,2,1,0:T(4,128)S(1)}, u32[]{:S(2)}, u32[]{:S(2)}) collective-permute-start(f32[16,12,4,128]{3,2,1,0:T(4,128)S(1)} %divide_add_fusion), channel_id=1, source_target_pairs={{1,0},{2,1},{3,2},{0,3},{5,4},{6,5},{7,6},{4,7},{9,8},{10,9},{11,1... | collective-permute-start | bytes 1179656 | tf_op jit(solution)/shard_map/ppermute | solution.py:126
  198.8 10.9 %collective-permute-start.28 = (f32[16,12,4,128]{3,2,1,0:T(4,128)S(1)}, f32[16,12,4,128]{3,2,1,0:T(4,128)S(1)}, u32[]{:S(2)}, u32[]{:S(2)}) collective-permute-start(f32[16,12,4,128]{3,2,1,0:T(4,128)S(1)} %divide_add_fusion), channel_id=1, source_target_pairs={{0,1},{1,2},{2,3},{3,0},{4,5},{5,6},{6,7},{7,4},{8,9},{9,10},{10,1... | collective-permute-start | bytes 1179656 | tf_op jit(solution)/shard_map/ppermute | solution.py:124
  200.7 11.0 %collective-permute-start.27 = (f32[16,1,4,128]{3,2,1,0:T(4,128)S(1)}, f32[16,1,4,128]{3,2,1,0:T(4,128)S(1)}, u32[]{:S(2)}, u32[]{:S(2)}) collective-permute-start(f32[16,1,4,128]{3,2,1,0:T(4,128)S(1)} %get-tuple-element.22), channel_id=1, source_target_pairs={{4,0},{8,4},{12,8},{16,12},{20,16},{24,20},{28,24},{32,28},{36,32}... | collective-permute-start | bytes 98312 | tf_op jit(solution)/shard_map/ppermute | solution.py:27
  202.7 9.1 %collective-permute-start.26 = (f32[16,1,4,128]{3,2,1,0:T(4,128)S(1)}, f32[16,1,4,128]{3,2,1,0:T(4,128)S(1)}, u32[]{:S(2)}, u32[]{:S(2)}) collective-permute-start(f32[16,1,4,128]{3,2,1,0:T(4,128)S(1)} %get-tuple-element.21), channel_id=1, source_target_pairs={{0,4},{4,8},{8,12},{12,16},{16,20},{20,24},{24,28},{28,32},{32,36}... | collective-permute-start | bytes 98312 | tf_op jit(solution)/shard_map/ppermute | solution.py:25
  209.7 2.8 copy-start.2
  209.7 11.0 %collective-permute-start.29 = (f32[16,12,4,128]{3,2,1,0:T(4,128)S(1)}, f32[16,12,4,128]{3,2,1,0:T(4,128)}, u32[]{:S(2)}, u32[]{:S(2)}) collective-permute-start(f32[16,12,4,128]{3,2,1,0:T(4,128)S(1)} %collective-permute-done.28), channel_id=1, source_target_pairs={{0,1},{1,2},{2,3},{3,0},{4,5},{5,6},{6,7},{7,4},{8,9},{9,10},{10,1... | collective-permute-start | bytes 1179656 | tf_op jit(solution)/shard_map/ppermute | solution.py:124
